TPU v7x, 256 devices: a whole 4x4x8 slice. The times are simulated.
256 devices in a mesh: dp: 16 (over z, core), mp: 16 (over y, x).
Axes of the slice: x: 4, y: 4, z: 8, core: 2. Of those that a mesh axis runs over, the one named last changes fastest.
Arguments:
- activations: bfloat16 [16, 1024, 4096], P('dp'), may hold values from -6 to 6
- out_grads: bfloat16 [16, 1024, 8192], P('dp', None, 'mp'), may hold values from -0.1875 to 0.1875
- error_fb: bfloat16 [16, 4096, 8192], P('dp', None, 'mp'), may hold values from -6 to 6
- q_prev: float32 [8192, 128], P('mp'), may hold values from -0.0625 to 0.0625
Outputs:
- new_error: bfloat16 [16, 4096, 8192], P('dp', None, 'mp')
- q_new: float32 [8192, 128], P('mp')
All inputs are finite; a program needn't handle non-finite values.
Results may differ from a plain program's by a relative error of at most 0.001.
Values sent between devices are 32-bit elements; how exact they have to be, the bound alone decides.
A program may use at most 128 MiB of HBM per device.

v0:
```python
import jax
import jax.numpy as jnp
from jax import lax
from jax.sharding import PartitionSpec as P


def orthonormal(p_part, gram):
    chol = jnp.linalg.cholesky(gram)
    return lax.linalg.triangular_solve(chol, p_part, left_side=False, lower=True, transpose_a=True)


def self_gram(p_part):
    return jnp.dot(p_part.T, p_part, precision=lax.Precision.HIGHEST)


def per_device(activations, out_grads, error_fb, q_prev):
    grad_full = lax.dot_general(
        activations[0], out_grads[0], (((0,), (0,)), ((), ())), preferred_element_type=jnp.float32
    )
    merged = grad_full + error_fb[0].astype(jnp.float32)
    p_local = jnp.dot(merged, q_prev, precision=lax.Precision.HIGHEST)
    p_sum = lax.psum(p_local, ("dp", "mp"))
    p_hat = orthonormal(p_sum, self_gram(p_sum))
    q_local = lax.dot_general(
        merged, p_hat, (((0,), (0,)), ((), ())), precision=lax.Precision.HIGHEST
    )
    q_new = lax.psum(q_local, "dp") / lax.axis_size("dp")
    approx = jnp.dot(p_hat, q_new.T, precision=lax.Precision.HIGHEST)
    new_error = (merged - approx).astype(jnp.bfloat16)[None]
    return (new_error, q_new)


def solution(mesh):
    placed = (P("dp", None, None), P("dp", None, "mp"), P("dp", None, "mp"), P("mp", None))
    return jax.shard_map(
        per_device,
        mesh=mesh,
        in_specs=placed,
        out_specs=(P("dp", None, "mp"), P("mp", None)),
        check_vma=False,
    )
```

profile of v0, /device:TPU:1, one launch (start us, length us, event | category | flops | bytes accessed | tf_op | source)
XLA Modules:
  0.0 475.6 jit_solution(18077918757856505209)
XLA Ops:
  7.2 0.0 copy-start
  7.2 0.0 copy-start.5
  7.2 0.0 all-reduce.3.cloned.1.call-start
  7.2 1.2 copy-done
  8.4 12.1 %convert_add_fusion = f32[4096,512]{1,0:T(8,128)S(1)} fusion(bf16[1,1024,4096]{2,1,0:T(8,128)(2,1)} %param.4, bf16[1,4096,512]{2,1,0:T(8,128)(2,1)} %param.6, bf16[1,1024,512]{2,1,0:T(8,128)(2,1)S(1)} %copy-done), kind=kOutput, calls=%fused_computation | convolution fusion | flops 4299161600 | bytes 22020096 | tf_op jit(solution)/shard_map/dot_general | solution.py:17
  20.5 0.0 copy-start.1
  20.6 3.2 copy-done.1
  23.8 0.0 copy-done.5
  23.8 8.1 %fusion.10 = f32[4096,128]{1,0:T(8,128)} fusion(f32[4096,512]{1,0:T(8,128)S(1)} %convert_add_fusion, f32[512,128]{1,0:T(8,128)S(1)} %copy-done.5), kind=kOutput, calls=%fused_computation.17 | convolution fusion | flops 3221225472 | bytes 10747904 | tf_op jit(solution)/shard_map/dot_general | solution.py:21
  31.8 0.0 all-reduce.3.cloned.1.call-update
  31.9 0.2 all-reduce.5.cloned.1.call-start
  32.1 265.9 %all-reduce.3.cloned.1.call-done = f32[4096,128]{1,0:T(8,128)} async-done(((f32[4096,128]{1,0:T(8,128)}), f32[4096,128]{1,0:T(8,128)}) %all-reduce.3.cloned.1.call-update) | async-done | bytes 2097168 | tf_op jit(solution)/shard_map/psum | solution.py:22
  298.0 0.0 copy-start.2
  298.0 5.8 %fusion.11 = f32[128,128]{1,0:T(8,128)S(1)} fusion(f32[4096,128]{1,0:T(8,128)} %all-reduce.3.cloned.1.call-done), kind=kOutput, calls=%fused_computation.18 | convolution fusion | flops 805306368 | bytes 2162688 | tf_op jit(solution)/shard_map/dot_general | solution.py:13
  303.8 0.1 copy.6
  303.9 11.7 %cholesky.16 = f32[128,128]{1,0:T(8,128)S(1)} custom-call(f32[128,128]{1,0:T(8,128)S(1)} %fusion.9), custom_call_target="Cholesky" | custom-call | tf_op jit(solution)/shard_map/jit(cholesky)/cholesky | solution.py:8
  315.7 0.6 compare_reduce_fusion
  316.3 0.7 fusion.6
  317.0 9.8 %custom-call.6 = f32[1,128,128]{1,2,0:T(8,128)S(1)} custom-call(f32[1,128,128]{2,1,0:T(8,128)S(1)} %fusion.6), custom_call_target="InvertDiagBlocksLowerTriangular" | custom-call | tf_op jit(solution)/shard_map/triangular_solve | solution.py:9
  326.8 0.0 copy-done.2
  326.8 1.8 fusion.7
  328.6 0.0 copy-start.3
  328.6 1.4 copy-done.3
  330.0 16.2 %fusion.12 = f32[512,128]{1,0:T(8,128)} fusion(f32[4096,512]{1,0:T(8,128)} %copy-done.1, f32[4096,128]{1,0:T(8,128)S(1)} %fusion.7), kind=kOutput, calls=%fused_computation.19 | convolution fusion | flops 3221225472 | bytes 10747904 | tf_op jit(solution)/shard_map/dot_general | solution.py:24
  346.1 0.0 all-reduce.5.cloned.1.call-update
  346.2 110.5 %all-reduce.5.cloned.1.call-done = f32[512,128]{1,0:T(8,128)} async-done(((f32[512,128]{1,0:T(8,128)}), f32[512,128]{1,0:T(8,128)}) %all-reduce.5.cloned.1.call-update) | async-done | bytes 262160 | tf_op jit(solution)/shard_map/psum | solution.py:27
  456.7 1.0 broadcast_multiply_fusion
  457.6 0.0 copy-start.4
  457.7 11.2 %fusion.4 = bf16[1,4096,512]{2,1,0:T(8,128)(2,1)} fusion(f32[4096,512]{1,0:T(8,128)} %copy-done.1, f32[4096,128]{1,0:T(8,128)} %copy-done.3, f32[512,128]{1,0:T(8,128)S(1)} %broadcast_multiply_fusion), kind=kOutput, calls=%fused_computation.4 | convolution fusion | flops 3225419776 | bytes 14942208 | tf_op jit(solution)/shard_map/dot_general | solution.py:28
  468.8 0.0 copy-done.4
  (2 shorter events, 0.0 us)
Async XLA Ops:
  7.2 1.2 copy-start
  7.2 16.6 %copy-start.5 = (f32[512,128]{1,0:T(8,128)S(1)}, f32[512,128]{1,0:T(8,128)}, u32[]{:S(2)}) copy-start(f32[512,128]{1,0:T(8,128)} %param.7) | copy-start | bytes 786436
  7.2 290.8 %all-reduce.3.cloned.1.call-start = ((), (), s32[]{:S(2)}) async-start(), calls=%async_computation | async-start | bytes 4194304 | tf_op jit(solution)/shard_map/psum | solution.py:22
  20.5 3.2 copy-start.1
  31.9 424.8 %all-reduce.5.cloned.1.call-start = ((), (), s32[]{:S(2)}) async-start(), calls=%async_computation.1 | async-start | bytes 524288 | tf_op jit(solution)/shard_map/psum | solution.py:27
  298.0 28.8 %copy-start.2 = (f32[4096,128]{1,0:T(8,128)S(1)}, f32[4096,128]{1,0:T(8,128)}, u32[]{:S(2)}) copy-start(f32[4096,128]{1,0:T(8,128)} %all-reduce.3.cloned.1.call-done) | copy-start | bytes 6291460
  328.6 1.4 copy-start.3
  457.6 11.2 %copy-start.4 = (f32[512,128]{1,0:T(8,128)}, f32[512,128]{1,0:T(8,128)S(1)}, u32[]{:S(2)}) copy-start(f32[512,128]{1,0:T(8,128)S(1)} %broadcast_multiply_fusion) | copy-start | bytes 786436
Sparse Core Ops, SparseCore 0:
  32.0 265.9 all-reduce.2
  346.3 110.3 all-reduce.4
where the time goes:
time: 476 us
  waiting for transfers between devices  376 us (79%)
  matrix products  55.1 us (12%)
  other arithmetic  23.8 us (5%)
  between operations  14.1 us (3%)
  local copies, waits for them, and re-layouts  5.86 us (1%)
    psum x1, waiting for transfers between devices, per_device(): p_sum = lax.psum(p_local, ('dp', 'mp'))  266 us
    psum x1, waiting for transfers between devices, per_device(): q_new = lax.psum(q_local, 'dp') / lax.axis_size('dp')  111 us
    dot_general x1, matrix products, per_device(): lax.dot_general(merged, p_hat, (((0,), (0,)), ((), ())), precision=lax.Pr...  16.2 us
    another operation x3, other arithmetic, orthonormal(): chol = jnp.linalg.cholesky(gram)  12.4 us
    dot_general x1, matrix products, per_device(): lax.dot_general(activations[0], out_grads[0], (((0,), (0,)), ((), ())), p...  12.1 us
    dot_general x1, matrix products, per_device(): approx = jnp.dot(p_hat, q_new.T, precision=lax.Precision.HIGHEST)  11.2 us
    another operation x2, other arithmetic, orthonormal(): lax.linalg.triangular_solve(chol, p_part, left_side=False, lower=True, tr...  10.5 us
  transfers between devices with their start and end apart: 2, of which 2 were waited for; matrix products, arithmetic and copies ran while one was open for 0% of the time, Pallas kernels for 0%

commit v1 on v0

--- a/solution.py
+++ b/solution.py
@@ -19,7 +19,8 @@
     )
     merged = grad_full + error_fb[0].astype(jnp.float32)
     p_local = jnp.dot(merged, q_prev, precision=lax.Precision.HIGHEST)
-    p_sum = lax.psum(p_local, ("dp", "mp"))
+    half = lax.psum(p_local, "mp")
+    p_sum = lax.psum(half, "dp")
     p_hat = orthonormal(p_sum, self_gram(p_sum))
     q_local = lax.dot_general(
         merged, p_hat, (((0,), (0,)), ((), ())), precision=lax.Precision.HIGHEST

time: 476 us -> 432 us (0.908)
  waiting for transfers between devices: 376 us -> 333 us
    psum x1 -> x2, waiting for transfers between devices: 266 us -> 222 us  [the longest x1 118 us: per_device(): p_sum = lax.psum(half, 'dp')]
  transfers between devices with their start and end apart: 2 -> 3, of which waited for: 2 -> 3; matrix products, arithmetic and copies ran while one was open for 0% -> 0% of each run, Pallas kernels for 0% -> 0%
where the time goes in v1:
time: 432 us
  waiting for transfers between devices  333 us (77%)
  matrix products  55.1 us (13%)
  other arithmetic  23.8 us (6%)
  between operations  13.9 us (3%)
  local copies, waits for them, and re-layouts  5.86 us (1%)
    psum x1, waiting for transfers between devices, per_device(): p_sum = lax.psum(half, 'dp')  118 us
    psum x1, waiting for transfers between devices, per_device(): q_new = lax.psum(q_local, 'dp') / lax.axis_size('dp')  111 us
    psum x1, waiting for transfers between devices, per_device(): half = lax.psum(p_local, 'mp')  104 us
    dot_general x1, matrix products, per_device(): lax.dot_general(merged, p_hat, (((0,), (0,)), ((), ())), precision=lax.Pr...  16.2 us
    another operation x3, other arithmetic, orthonormal(): chol = jnp.linalg.cholesky(gram)  12.4 us
    dot_general x1, matrix products, per_device(): lax.dot_general(activations[0], out_grads[0], (((0,), (0,)), ((), ())), p...  12.1 us
    dot_general x1, matrix products, per_device(): approx = jnp.dot(p_hat, q_new.T, precision=lax.Precision.HIGHEST)  11.1 us
    another operation x2, other arithmetic, orthonormal(): lax.linalg.triangular_solve(chol, p_part, left_side=False, lower=True, tr...  10.5 us
  transfers between devices with their start and end apart: 3, of which 3 were waited for; matrix products, arithmetic and copies ran while one was open for 0% of the time, Pallas kernels for 0%

profile of v1, /device:TPU:1, one launch (start us, length us, event | category | flops | bytes accessed | tf_op | source)
XLA Modules:
  0.0 431.6 jit_solution(10779407103708706681)
XLA Ops:
  7.2 0.0 copy-start
  7.2 0.0 copy-start.5
  7.2 0.0 all-reduce.4.cloned.1.call-start
  7.2 1.2 copy-done
  8.4 12.1 %convert_add_fusion = f32[4096,512]{1,0:T(8,128)S(1)} fusion(bf16[1,1024,4096]{2,1,0:T(8,128)(2,1)} %param.4, bf16[1,4096,512]{2,1,0:T(8,128)(2,1)} %param.6, bf16[1,1024,512]{2,1,0:T(8,128)(2,1)S(1)} %copy-done), kind=kOutput, calls=%fused_computation | convolution fusion | flops 4299161600 | bytes 22020096 | tf_op jit(solution)/shard_map/dot_general | solution.py:17
  20.5 0.0 copy-start.1
  20.6 3.2 copy-done.1
  23.8 0.0 copy-done.5
  23.8 8.1 %fusion.10 = f32[4096,128]{1,0:T(8,128)} fusion(f32[4096,512]{1,0:T(8,128)S(1)} %convert_add_fusion, f32[512,128]{1,0:T(8,128)S(1)} %copy-done.5), kind=kOutput, calls=%fused_computation.17 | convolution fusion | flops 3221225472 | bytes 10747904 | tf_op jit(solution)/shard_map/dot_general | solution.py:21
  31.8 0.0 all-reduce.4.cloned.1.call-update
  31.9 0.0 all-reduce.6.cloned.1.call-start
  31.9 103.7 %all-reduce.4.cloned.1.call-done = f32[4096,128]{1,0:T(8,128)} async-done(((f32[4096,128]{1,0:T(8,128)}), f32[4096,128]{1,0:T(8,128)}) %all-reduce.4.cloned.1.call-update) | async-done | bytes 2097168 | tf_op jit(solution)/shard_map/psum | solution.py:22
  135.6 0.0 all-reduce.6.cloned.1.call-update
  135.6 0.2 all-reduce.8.cloned.1.call-start
  135.8 118.2 %all-reduce.6.cloned.1.call-done = f32[4096,128]{1,0:T(8,128)} async-done(((f32[4096,128]{1,0:T(8,128)}), f32[4096,128]{1,0:T(8,128)}) %all-reduce.6.cloned.1.call-update) | async-done | bytes 2097168 | tf_op jit(solution)/shard_map/psum | solution.py:23
  254.1 5.8 %fusion.11 = f32[128,128]{1,0:T(8,128)S(1)} fusion(f32[4096,128]{1,0:T(8,128)} %all-reduce.6.cloned.1.call-done), kind=kOutput, calls=%fused_computation.18 | convolution fusion | flops 805306368 | bytes 2162688 | tf_op jit(solution)/shard_map/dot_general | solution.py:13
  259.9 0.1 copy.6
  260.0 11.7 %cholesky.16 = f32[128,128]{1,0:T(8,128)S(1)} custom-call(f32[128,128]{1,0:T(8,128)S(1)} %fusion.9), custom_call_target="Cholesky" | custom-call | tf_op jit(solution)/shard_map/jit(cholesky)/cholesky | solution.py:8
  271.7 0.6 compare_reduce_fusion
  272.4 0.7 fusion.6
  273.1 9.8 %custom-call.6 = f32[1,128,128]{1,2,0:T(8,128)S(1)} custom-call(f32[1,128,128]{2,1,0:T(8,128)S(1)} %fusion.6), custom_call_target="InvertDiagBlocksLowerTriangular" | custom-call | tf_op jit(solution)/shard_map/triangular_solve | solution.py:9
  282.9 0.0 copy-done.2
  282.9 1.8 fusion.7
  284.7 0.0 copy-start.3
  284.7 1.4 copy-done.3
  286.1 16.2 %fusion.12 = f32[512,128]{1,0:T(8,128)} fusion(f32[4096,512]{1,0:T(8,128)} %copy-done.1, f32[4096,128]{1,0:T(8,128)S(1)} %fusion.7), kind=kOutput, calls=%fused_computation.19 | convolution fusion | flops 3221225472 | bytes 10747904 | tf_op jit(solution)/shard_map/dot_general | solution.py:25
  302.2 0.0 all-reduce.8.cloned.1.call-update
  302.2 110.6 %all-reduce.8.cloned.1.call-done = f32[512,128]{1,0:T(8,128)} async-done(((f32[512,128]{1,0:T(8,128)}), f32[512,128]{1,0:T(8,128)}) %all-reduce.8.cloned.1.call-update) | async-done | bytes 262160 | tf_op jit(solution)/shard_map/psum | solution.py:28
  412.9 1.0 broadcast_multiply_fusion
  413.9 0.0 copy-start.4
  413.9 11.1 %fusion.4 = bf16[1,4096,512]{2,1,0:T(8,128)(2,1)} fusion(f32[4096,512]{1,0:T(8,128)} %copy-done.1, f32[4096,128]{1,0:T(8,128)} %copy-done.3, f32[512,128]{1,0:T(8,128)S(1)} %broadcast_multiply_fusion), kind=kOutput, calls=%fused_computation.4 | convolution fusion | flops 3225419776 | bytes 14942208 | tf_op jit(solution)/shard_map/dot_general | solution.py:29
  425.0 0.0 copy-done.4
  (3 shorter events, 0.0 us)
Async XLA Ops:
  7.2 1.2 copy-start
  7.2 16.6 %copy-start.5 = (f32[512,128]{1,0:T(8,128)S(1)}, f32[512,128]{1,0:T(8,128)}, u32[]{:S(2)}) copy-start(f32[512,128]{1,0:T(8,128)} %param.7) | copy-start | bytes 786436
  7.2 128.4 %all-reduce.4.cloned.1.call-start = ((), (), s32[]{:S(2)}) async-start(), calls=%async_computation | async-start | bytes 4194304 | tf_op jit(solution)/shard_map/psum | solution.py:22
  20.5 3.2 copy-start.1
  31.9 222.2 %all-reduce.6.cloned.1.call-start = ((), (), s32[]{:S(2)}) async-start(), calls=%async_computation.1 | async-start | bytes 4194304 | tf_op jit(solution)/shard_map/psum | solution.py:23
  135.6 277.3 %all-reduce.8.cloned.1.call-start = ((), (), s32[]{:S(2)}) async-start(), calls=%async_computation.2 | async-start | bytes 524288 | tf_op jit(solution)/shard_map/psum | solution.py:28
  254.1 28.8 %copy-start.2 = (f32[4096,128]{1,0:T(8,128)S(1)}, f32[4096,128]{1,0:T(8,128)}, u32[]{:S(2)}) copy-start(f32[4096,128]{1,0:T(8,128)} %all-reduce.6.cloned.1.call-done) | copy-start | bytes 6291460
  284.7 1.4 copy-start.3
  413.9 11.2 %copy-start.4 = (f32[512,128]{1,0:T(8,128)}, f32[512,128]{1,0:T(8,128)S(1)}, u32[]{:S(2)}) copy-start(f32[512,128]{1,0:T(8,128)S(1)} %broadcast_multiply_fusion) | copy-start | bytes 786436
Sparse Core Ops, SparseCore 0:
  32.0 103.5 all-reduce.3
  137.9 116.0 all-reduce.5
  302.4 110.4 all-reduce.7
